TPU v7x, 256 devices: a whole 4x4x8 slice. The times are simulated.
256 devices in a mesh: dp: 4 (over y_hi, core), seq: 8 (over z), head: 8 (over x, y_lo).
Axes of the slice: x: 4, y: 4 (y_hi: 2, y_lo: 2; y = y_hi * 2 + y_lo), z: 8, core: 2. Of those that a mesh axis runs over, the one named last changes fastest.
Arguments:
- tokens: bfloat16 [4, 8192, 512], P('dp', ('seq', 'head')), may hold values from -800 to 800
- bin_ids: int32 [4, 8192], P('dp'), may hold values from 0 to 127, never falling along the last dimension, each value on 1 to 256 neighbouring positions
- pattern: int32 [4, 64, 9], P('dp'), may hold values from 0 to 63, as said below
- w_qkv: bfloat16 [512, 1536], replicated, may hold values from -3.2 to 3.2
- w_out: bfloat16 [512, 512], replicated, may hold values from -5 to 5
- head_bias: float32 [8], replicated, may hold values from -3 to 400
- grad_output: bfloat16 [4, 8192, 512], P('dp', ('seq', 'head')), may hold values from -6 to 6
Outputs:
- output: bfloat16 [4, 8192, 512], P('dp', ('seq', 'head'))
- grad_tokens: bfloat16 [4, 8192, 512], P('dp', ('seq', 'head'))
- grad_w_qkv: float32 [512, 1536], P(None, 'head')
- grad_w_out: float32 [512, 512], P('head')
Inputs may be any that keep to these rules, and one draw needn't show every extreme that they name: `pattern`: row i of sequence b lists (i + o) mod 64 for the 9 offsets o of sequence b, in the same order in every row: 0, 1, -1, then distinct a from 2 to 31, then their negatives. So block J is in row I exactly when I is in row J. `bin_ids`: bin numbers never fall along a sequence.
All inputs are finite; a program needn't handle non-finite values.
Results may differ from a plain program's by a relative error of at most 0.01.
Values may be sent and summed in bfloat16 or wider, within the bound.
A program may use at most 64 MiB of HBM per device.

v0:
```python
import math
import jax
import jax.numpy as jnp
from jax import lax
from jax.sharding import PartitionSpec as P

D = 512
HEADS = 8
HD = 64
BLK = 128
NNZ = 9
EPSILON = 1e-05


def normalize(token_rows):
    widened = token_rows.astype(jnp.float32)
    spread = jnp.sqrt(jnp.mean(widened * widened, axis=-1, keepdims=True) + EPSILON)
    return (widened / spread, spread)


def query_scores(query_blk, key_blk, bin_query, bin_key, bias_local, factor):
    raw_scores = jnp.einsum(
        "gqhe,gnkhe->ghqnk", query_blk, key_blk, preferred_element_type=jnp.float32
    )
    same_bin = (bin_query[:, None, :, None, None] == bin_key[:, None, None, :, :]).astype(
        jnp.float32
    )
    scores = raw_scores * factor + bias_local[None, :, None, None, None] * same_bin
    return scores.reshape(scores.shape[0], scores.shape[1], scores.shape[2], -1)


def body(tokens, bin_ids, pattern, w_qkv, w_out, head_bias, grad_output):
    tok_rows = tokens.shape[1]
    head_parts = lax.axis_size("head")
    local_heads = HEADS // head_parts
    seq_rows = tok_rows * head_parts
    seq_length = bin_ids.shape[1]
    blocks_all = seq_length // BLK
    local_blocks = seq_rows // BLK
    group_size = math.gcd(local_blocks, 4)
    group_count = local_blocks // group_size
    factor = 1.0 / math.sqrt(HD)
    seq_pos = lax.axis_index("seq")
    head_pos = lax.axis_index("head")
    first_block = seq_pos * local_blocks
    key_lists = lax.dynamic_slice_in_dim(pattern[0], first_block, local_blocks, 0)
    bin_table = bin_ids[0].reshape(blocks_all, BLK)
    bin_local = lax.dynamic_slice_in_dim(bin_table, first_block, local_blocks, 0)
    bias_local = lax.dynamic_slice_in_dim(head_bias, head_pos * local_heads, local_heads, 0)

    def grouped(array):
        return array.reshape((group_count, group_size) + array.shape[1:])

    normed, spread = normalize(tokens[0])
    hidden = normed.astype(jnp.bfloat16)
    packed = jnp.dot(hidden, w_qkv, preferred_element_type=jnp.float32).astype(jnp.bfloat16)
    packed = packed.reshape(tok_rows, HEADS, 3 * HD)
    packed_heads = lax.all_to_all(packed, "head", split_axis=1, concat_axis=0, tiled=True)
    queries = packed_heads[:, :, :HD]
    pair_local = packed_heads[:, :, HD:]
    pair_all = lax.all_gather(pair_local, "seq", axis=0, tiled=True)
    pair_table = pair_all.reshape(blocks_all, BLK, local_heads, 2 * HD)
    query_blocks = queries.reshape(local_blocks, BLK, local_heads, HD)

    def forward_group(entries):
        query_blk, key_rows, bin_query = entries
        pair_blk = jnp.take(pair_table, key_rows, axis=0)
        bin_key = jnp.take(bin_table, key_rows, axis=0)
        scores = query_scores(query_blk, pair_blk[..., :HD], bin_query, bin_key, bias_local, factor)
        row_max = jnp.max(scores, axis=-1, keepdims=True)
        log_total = row_max + jnp.log(jnp.sum(jnp.exp(scores - row_max), axis=-1, keepdims=True))
        probs = jnp.exp(scores - log_total).astype(jnp.bfloat16)
        value_flat = pair_blk[..., HD:].reshape(group_size, NNZ * BLK, local_heads, HD)
        attended = jnp.einsum(
            "ghqm,gmhe->gqhe", probs, value_flat, preferred_element_type=jnp.float32
        )
        return (attended.astype(jnp.bfloat16), log_total[..., 0])

    attended, log_blocks = lax.map(
        forward_group, (grouped(query_blocks), grouped(key_lists), grouped(bin_local))
    )
    attended_heads = attended.reshape(seq_rows, local_heads, HD)
    log_blocks = log_blocks.reshape(local_blocks, local_heads, BLK)
    attended_tok = lax.all_to_all(
        attended_heads, "head", split_axis=0, concat_axis=1, tiled=True
    ).reshape(tok_rows, D)
    result = jnp.dot(attended_tok, w_out, preferred_element_type=jnp.float32).astype(jnp.bfloat16)
    grad_rows = grad_output[0]
    grad_att = jnp.dot(grad_rows, w_out.T, preferred_element_type=jnp.float32).astype(jnp.bfloat16)
    grad_heads = lax.all_to_all(
        grad_att.reshape(tok_rows, HEADS, HD), "head", split_axis=1, concat_axis=0, tiled=True
    )
    delta_rows = jnp.sum(
        grad_heads.astype(jnp.float32) * attended_heads.astype(jnp.float32), axis=-1
    )
    delta_blocks = delta_rows.reshape(local_blocks, BLK, local_heads).swapaxes(1, 2)
    grad_blocks = grad_heads.reshape(local_blocks, BLK, local_heads, HD)

    def query_core(entries):
        query_blk, grad_blk, log_blk, delta_blk, key_rows, bin_query = entries
        pair_blk = jnp.take(pair_table, key_rows, axis=0)
        bin_key = jnp.take(bin_table, key_rows, axis=0)
        scores = query_scores(query_blk, pair_blk[..., :HD], bin_query, bin_key, bias_local, factor)
        probs = jnp.exp(scores - log_blk[..., None])
        value_flat = pair_blk[..., HD:].reshape(group_size, NNZ * BLK, local_heads, HD)
        key_flat = pair_blk[..., :HD].reshape(group_size, NNZ * BLK, local_heads, HD)
        grad_prob = jnp.einsum(
            "gqhe,gmhe->ghqm", grad_blk, value_flat, preferred_element_type=jnp.float32
        )
        grad_score = (probs * (grad_prob - delta_blk[..., None]) * factor).astype(jnp.bfloat16)
        grad_query = jnp.einsum(
            "ghqm,gmhe->gqhe", grad_score, key_flat, preferred_element_type=jnp.float32
        )
        return (grad_query.astype(jnp.bfloat16), grad_score, probs)

    query_entries = (
        grouped(query_blocks),
        grouped(grad_blocks),
        grouped(log_blocks),
        grouped(delta_blocks),
        grouped(key_lists),
        grouped(bin_local),
    )

    def scatter_step(carried, entries):
        query_blk, grad_blk = (entries[0], entries[1])
        key_rows = entries[4]
        grad_query, grad_score, probs = query_core(entries)
        key_part = jnp.einsum(
            "ghqm,gqhe->gmhe", grad_score, query_blk, preferred_element_type=jnp.float32
        )
        value_part = jnp.einsum(
            "ghqm,gqhe->gmhe",
            probs.astype(jnp.bfloat16),
            grad_blk,
            preferred_element_type=jnp.float32,
        )
        both_parts = jnp.concatenate([key_part, value_part], axis=-1)
        both_parts = both_parts.reshape(group_size * NNZ, BLK, local_heads, 2 * HD)
        carried = carried.at[key_rows.reshape(-1)].add(both_parts)
        return (carried, grad_query)

    empty_sum = jnp.zeros((blocks_all, BLK, local_heads, 2 * HD), jnp.float32)
    pair_sums, grad_queries = lax.scan(scatter_step, empty_sum, query_entries)
    own_pairs = lax.psum_scatter(
        pair_sums.reshape(seq_length, local_heads, 2 * HD), "seq", scatter_dimension=0, tiled=True
    )
    grad_pairs = own_pairs.astype(jnp.bfloat16)
    grad_packed_heads = jnp.concatenate(
        [grad_queries.reshape(seq_rows, local_heads, HD), grad_pairs], axis=-1
    )
    grad_packed = lax.all_to_all(
        grad_packed_heads, "head", split_axis=0, concat_axis=1, tiled=True
    ).reshape(tok_rows, 3 * D)
    grad_hidden = jnp.dot(grad_packed, w_qkv.T, preferred_element_type=jnp.float32)
    inner = jnp.mean(grad_hidden * normed, axis=-1, keepdims=True)
    grad_input = ((grad_hidden - normed * inner) / spread).astype(jnp.bfloat16)
    local_qkv = jnp.einsum("td,tc->dc", hidden, grad_packed, preferred_element_type=jnp.float32)
    local_out = jnp.einsum("td,tc->dc", grad_rows, attended_tok, preferred_element_type=jnp.float32)
    total_qkv, total_out = lax.psum((local_qkv, local_out), ("dp", "seq", "head"))
    own_qkv = lax.dynamic_slice_in_dim(
        total_qkv, head_pos * local_heads * 3 * HD, local_heads * 3 * HD, 1
    )
    own_out = lax.dynamic_slice_in_dim(total_out, head_pos * local_heads * HD, local_heads * HD, 1)
    return (result[None], grad_input[None], own_qkv, own_out.T)


def solution(mesh):
    return jax.shard_map(
        body,
        mesh=mesh,
        in_specs=(
            P("dp", ("seq", "head"), None),
            P("dp", None),
            P("dp", None, None),
            P(),
            P(),
            P(),
            P("dp", ("seq", "head"), None),
        ),
        out_specs=(
            P("dp", ("seq", "head"), None),
            P("dp", ("seq", "head"), None),
            P(None, "head"),
            P("head", None),
        ),
        check_vma=False,
    )
```

profile of v0, /device:TPU:2, one launch (start us, length us, event | category | flops | bytes accessed | tf_op | source)
XLA Modules:
  0.0 558.7 jit_solution(6286347255980764140)
XLA Ops:
  10.6 12.6 %all_to_all.63 = bf16[128,8,192]{0,2,1:T(8,128)(2,1)S(1)} all-to-all(bf16[128,8,192]{0,2,1:T(8,128)(2,1)S(1)} %bitcast.271), channel_id=1, replica_groups=mesh['dp'=4,'seq'=8,'head'=8] {'head'}, dimensions={1} | all-to-all | bytes 786432 | tf_op jit(solution)/shard_map/all_to_all | solution.py:58
  25.1 4.8 all-to-all-start.2
  30.9 36.5 %all-gather.2.cloned.1.call-done = bf16[8192,1,128]{0,2,1:T(8,128)(2,1)} async-done(((bf16[1024,1,128]{0,2,1:T(8,128)(2,1)}), bf16[8192,1,128]{0,2,1:T(8,128)(2,1)}) %all-gather.2.cloned.1.call-update) | async-done | bytes 2097168 | tf_op jit(solution)/shard_map/all_gather | solution.py:61
  67.4 4.1 copy.119
  72.1 40.3 %while.24 = (s32[]{:T(128)}, bf16[2,4,128,1,64]{2,4,1,3,0:T(8,128)(2,1)}, f32[2,4,1,128]{3,1,2,0:T(4,128)}, s32[2,4,9]{2,1,0:T(4,128)S(1)}, bf16[64,128,1,128]{3...) while((s32[]{:T(128)}, ...), condition=%wide.region_4.7_spmd, body=%wide.region_1.6_spmd.sunk | while | flops 156931296 | bytes 39141280 | solution.py:79
  73.5 3.4 gather_fusion
  80.7 3.7 fusion.80
  86.2 3.1 copy.153
  93.6 3.4 gather_fusion
  100.8 3.7 fusion.80
  106.3 3.1 copy.153
  116.5 86.1 %while.25 = (s32[]{:T(128)}, f32[64,128,1,128]{3,1,0,2:T(8,128)}, bf16[2,4,128,1,64]{2,4,1,3,0:T(8,128)(2,1)}, s32[2,4,9]{2,1,0:T(4,128)S(1)}, bf16[2,4,128,1,64...) while((s32[]{:T(128)}, f32[64,128,1,128]{3,1,0,2:T(8,128)}, ...), condition=%wide.region_8.11_spmd, body=%wide.region_6.10_spmd.sunk | while | flops 385783744 | bytes 64560684 | solution.py:144
  133.0 4.2 select_add_fusion.3
  137.2 3.1 copy.155
  149.6 10.0 %scatter_fusion = f32[64,128,128]{2,1,0:T(8,128)} fusion(f32[64,128,128]{2,1,0:T(8,128)} %bitcast.263, s32[36]{0:T(128)S(1)} %copy-done.24, f32[36,128,128]{2,1,0:T(8,128)} %bitcast.257), kind=kCustom, calls=%fused_computation.4.clone.1 | custom fusion | flops 589824 | bytes 7078032 | tf_op jit(solution)/shard_map/while/body/eval_jaxpr/scatter-add | solution.py:140
  176.0 4.2 select_add_fusion.3
  180.2 3.1 copy.155
  192.5 10.0 %scatter_fusion = f32[64,128,128]{2,1,0:T(8,128)} fusion(f32[64,128,128]{2,1,0:T(8,128)} %bitcast.263, s32[36]{0:T(128)S(1)} %copy-done.24, f32[36,128,128]{2,1,0:T(8,128)} %bitcast.257), kind=kCustom, calls=%fused_computation.4.clone.1 | custom fusion | flops 589824 | bytes 7078032 | tf_op jit(solution)/shard_map/while/body/eval_jaxpr/scatter-add | solution.py:140
  207.7 5.7 %all-to-all-start.1 = ((bf16[8,2,4096]{2,1,0:T(2,128)(2,1)}), bf16[8,2,4096]{2,1,0:T(2,128)(2,1)S(1)}, u32[]{:S(2)}, u32[]{:S(2)}) async-start(bf16[8,2,4096]{2,1,0:T(2,128)(2,1)} %reshape.393), calls=%async_computation.1 | async-start | bytes 262144 | tf_op jit(solution)/shard_map/all_to_all | solution.py:84
  213.8 43.0 %reduce-scatter.2.cloned.1.call-done = f32[1024,1,128]{2,1,0:T(1,128)} async-done(((f32[8192,1,128]{2,1,0:T(1,128)}), f32[1024,1,128]{2,1,0:T(1,128)}) %reduce-scatter.2.cloned.1.call-update) | async-done | bytes 524304 | tf_op jit(solution)/shard_map/reduce_scatter | solution.py:145
  260.2 4.1 reduce.10
  265.6 5.7 %all-to-all-start.3 = ((bf16[8,2,12288]{2,1,0:T(2,128)(2,1)}), bf16[8,2,12288]{2,1,0:T(2,128)(2,1)S(1)}, u32[]{:S(2)}, u32[]{:S(2)}) async-start(bf16[8,2,12288]{2,1,0:T(2,128)(2,1)} %reshape.395), calls=%async_computation.4 | async-start | bytes 786432 | tf_op jit(solution)/shard_map/all_to_all | solution.py:152
  273.3 4.7 all-to-all-done.3
  285.3 263.5 %all-reduce.3.cloned.1.call-done = (f32[512,1536]{0,1:T(8,128)}, f32[512,512]{0,1:T(8,128)}) async-done(((f32[512,1536]{0,1:T(8,128)}, f32[512,512]{0,1:T(8,128)}), (f32[512,1536]{0,1:T(8,128)}, f32[512,512]{0,1:T(8,128)})) %all-reduce.3.cloned.1.call-update) | async-done | bytes 4194320 | tf_op jit(solution)/shard_map/psum | solution.py:160
  (224 shorter events, 104.4 us)
Async XLA Ops:
  7.2 60.2 %all-gather.2.cloned.1.call-start = ((), (), s32[]{:S(2)}) async-start(), calls=%async_computation.5 | async-start | bytes 2359296 | tf_op jit(solution)/shard_map/all_gather | solution.py:61
  9.0 15.1 %copy-start.6 = (bf16[512,512]{1,0:T(8,128)(2,1)S(1)}, bf16[512,512]{1,0:T(8,128)(2,1)}, u32[]{:S(2)}) copy-start(bf16[512,512]{1,0:T(8,128)(2,1)} %param.19) | copy-start | bytes 1572868
  9.0 15.1 %copy-start.17 = (bf16[1,128,512]{2,1,0:T(8,128)(2,1)S(1)}, bf16[1,128,512]{2,1,0:T(8,128)(2,1)}, u32[]{:S(2)}) copy-start(bf16[1,128,512]{2,1,0:T(8,128)(2,1)} %param.21) | copy-start | bytes 393220
  10.3 19.6 %copy-start.25 = (s32[1,64,9]{1,0,2:T(1,128)S(1)}, s32[1,64,9]{1,0,2:T(1,128)}, u32[]{:S(2)}) copy-start(s32[1,64,9]{1,0,2:T(1,128)} %param.17) | copy-start | bytes 6916
  10.4 19.8 %copy-start.28 = (f32[8]{0:T(128)S(1)}, f32[8]{0:T(128)}, u32[]{:S(2)}) copy-start(f32[8]{0:T(128)} %param.20) | copy-start | bytes 100
  10.4 20.4 %copy-start.3 = (s32[1,8192]{1,0:T(1,128)S(1)}, s32[1,8192]{1,0:T(1,128)}, u32[]{:S(2)}) copy-start(s32[1,8192]{1,0:T(1,128)} %param.16) | copy-start | bytes 98308
  25.1 87.3 %all-to-all-start.2 = ((bf16[128,8,64]{0,2,1:T(8,128)(2,1)}), bf16[128,8,64]{0,2,1:T(8,128)(2,1)S(1)}, u32[]{:S(2)}, u32[]{:S(2)}) async-start(bf16[128,8,64]{0,2,1:T(8,128)(2,1)} %bitcast.50), calls=%async_computation.2 | async-start | bytes 262144 | tf_op jit(solution)/shard_map/all_to_all | solution.py:90
  29.9 226.8 %reduce-scatter.2.cloned.1.call-start = ((), (), s32[]{:S(2)}) async-start(), calls=%async_computation.6 | async-start | bytes 4718592 | tf_op jit(solution)/shard_map/reduce_scatter | solution.py:145
  80.7 5.4 copy-start.22
  86.1 3.2 copy-start.23
  100.8 5.4 copy-start.22
  106.3 3.2 copy-start.23
  106.3 3.1 copy-start.10
  116.5 6.5 %copy-start.8 = (bf16[2,4,128,1,64]{2,4,1,3,0:T(8,128)(2,1)}, bf16[2,4,128,1,64]{2,4,1,3,0:T(8,128)(2,1)S(1)}, u32[]{:S(2)}) copy-start(bf16[2,4,128,1,64]{2,4,1,3,0:T(8,128)(2,1)S(1)} %get-tuple-element.496) | copy-start | bytes 393220 | tf_op jit(solution)/shard_map/while
  149.6 10.0 %copy-start.21 = (f32[2,4,1,128]{3,1,2,0:T(4,128)S(1)}, f32[2,4,1,128]{3,1,2,0:T(4,128)}, u32[]{:S(2)}) copy-start(f32[2,4,1,128]{3,1,2,0:T(4,128)} %copy-done.20) | copy-start | bytes 12292 | tf_op jit(solution)/shard_map/while
  159.5 6.5 %copy-start.8 = (bf16[2,4,128,1,64]{2,4,1,3,0:T(8,128)(2,1)}, bf16[2,4,128,1,64]{2,4,1,3,0:T(8,128)(2,1)S(1)}, u32[]{:S(2)}) copy-start(bf16[2,4,128,1,64]{2,4,1,3,0:T(8,128)(2,1)S(1)} %get-tuple-element.496) | copy-start | bytes 393220 | tf_op jit(solution)/shard_map/while
  192.5 10.0 %copy-start.21 = (f32[2,4,1,128]{3,1,2,0:T(4,128)S(1)}, f32[2,4,1,128]{3,1,2,0:T(4,128)}, u32[]{:S(2)}) copy-start(f32[2,4,1,128]{3,1,2,0:T(4,128)} %copy-done.20) | copy-start | bytes 12292 | tf_op jit(solution)/shard_map/while
  203.5 9.9 %copy-start.16 = (bf16[2,4,128,1,64]{2,4,1,3,0:T(8,128)(2,1)S(1)}, bf16[2,4,128,1,64]{2,4,1,3,0:T(8,128)(2,1)}, u32[]{:S(2)}) copy-start(bf16[2,4,128,1,64]{2,4,1,3,0:T(8,128)(2,1)} %get-tuple-element.119) | copy-start | bytes 393220
  207.7 57.9 %all-to-all-start.1 = ((bf16[8,2,4096]{2,1,0:T(2,128)(2,1)}), bf16[8,2,4096]{2,1,0:T(2,128)(2,1)S(1)}, u32[]{:S(2)}, u32[]{:S(2)}) async-start(bf16[8,2,4096]{2,1,0:T(2,128)(2,1)} %reshape.393), calls=%async_computation.1 | async-start | bytes 262144 | tf_op jit(solution)/shard_map/all_to_all | solution.py:84
  260.2 11.9 %copy-start.18 = (bf16[1,128,512]{2,1,0:T(8,128)(2,1)S(1)}, bf16[1,128,512]{2,1,0:T(8,128)(2,1)}, u32[]{:S(2)}) copy-start(bf16[1,128,512]{2,1,0:T(8,128)(2,1)} %param.21) | copy-start | bytes 393220
  265.6 12.4 %all-to-all-start.3 = ((bf16[8,2,12288]{2,1,0:T(2,128)(2,1)}), bf16[8,2,12288]{2,1,0:T(2,128)(2,1)S(1)}, u32[]{:S(2)}, u32[]{:S(2)}) async-start(bf16[8,2,12288]{2,1,0:T(2,128)(2,1)} %reshape.395), calls=%async_computation.4 | async-start | bytes 786432 | tf_op jit(solution)/shard_map/all_to_all | solution.py:152
  271.3 277.5 %all-reduce.3.cloned.1.call-start = ((), (), s32[]{:S(2)}) async-start(), calls=%async_computation.7 | async-start | bytes 8388608 | tf_op jit(solution)/shard_map/psum | solution.py:160
  273.3 6.2 %copy-start.13 = (bf16[1,128,512]{2,1,0:T(8,128)(2,1)S(1)}, bf16[1,128,512]{2,1,0:T(8,128)(2,1)}, u32[]{:S(2)}) copy-start(bf16[1,128,512]{2,1,0:T(8,128)(2,1)} %param.15) | copy-start | bytes 393220
  273.3 6.2 %copy-start.27 = (f32[128]{0:T(128)S(1)}, f32[128]{0:T(128)}, u32[]{:S(2)}) copy-start(f32[128]{0:T(128)} %copy-done.26) | copy-start | bytes 1540
  (27 other events, 43.4 us)
Sparse Core Ops, SparseCore 0:
  24.2 43.1 all-gather.1
  202.7 53.9 reduce-scatter.1
  281.9 266.7 all-reduce.2
where the time goes:
time: 561 us; the launch traced here: 559 us
  waiting for transfers between devices  348 us (62%)
  local copies, waits for them, and re-layouts  90.9 us (16%)
  other arithmetic  41.3 us (7%)
  matrix products  35.3 us (6%)
  starting transfers between devices  16.3 us (3%)
  between operations  14 us (2%)
  blocking collectives  12.6 us (2%)
    psum x1, waiting for transfers between devices, body(): lax.psum((local_qkv, local_out), ('dp', 'seq', 'head'))  264 us
    reduce_scatter x1, waiting for transfers between devices, body(): lax.psum_scatter(pair_sums.reshape(seq_length, local_heads, 2 * HD), 'seq...  43 us
    all_gather x1, waiting for transfers between devices, body(): pair_all = lax.all_gather(pair_local, 'seq', axis=0, tiled=True)  36.5 us
    scatter-add x2, other arithmetic, scatter_step(): carried = carried.at[key_rows.reshape(-1)].add(both_parts)  20 us
    dot_general x4, matrix products, query_scores(): jnp.einsum('gqhe,gnkhe->ghqnk', query_blk, key_blk, preferred_element_typ...  15.7 us
    all_to_all x1, blocking collectives, body(): lax.all_to_all(packed, 'head', split_axis=1, concat_axis=0, tiled=True)  12.6 us
    reshape x4, local copies, waits for them, and re-layouts, query_scores(): return scores.reshape(scores.shape[0], scores.shape[1], scores.shape[2], -1)  12.5 us
  transfers between devices with their start and end apart: 6, of which 4 were waited for; matrix products, arithmetic and copies ran while one was open for 10% of the time, Pallas kernels for 0%

commit v1 on v0

--- a/solution.py
+++ b/solution.py
@@ -58,7 +58,11 @@
     packed_heads = lax.all_to_all(packed, "head", split_axis=1, concat_axis=0, tiled=True)
     queries = packed_heads[:, :, :HD]
     pair_local = packed_heads[:, :, HD:]
-    pair_all = lax.all_gather(pair_local, "seq", axis=0, tiled=True)
+    size = lax.axis_size("seq")
+    repeats = [size if d == 0 else 1 for d in range(pair_local.ndim)]
+    pair_all = lax.all_to_all(
+        jnp.tile(pair_local, repeats), "seq", split_axis=0, concat_axis=0, tiled=True
+    )
     pair_table = pair_all.reshape(blocks_all, BLK, local_heads, 2 * HD)
     query_blocks = queries.reshape(local_blocks, BLK, local_heads, HD)
 

time: 561 us -> 597 us (1.064)
  local copies, waits for them, and re-layouts: 90.9 us -> 104 us
  waiting for transfers between devices: 348 us -> 357 us
  starting transfers between devices: 16.3 us -> 24.9 us
    all_to_all x0 -> x1, waiting for transfers between devices: none -> 47.8 us  [body(): lax.all_to_all(jnp.tile(pair_local, repeats), 'seq', split_axis=0, concat...]
    all_gather x1 -> x0, waiting for transfers between devices: 36.5 us -> none  [body(): pair_all = lax.all_gather(pair_local, 'seq', axis=0, tiled=True)]
    unnamed x33 -> x36, local copies, waits for them, and re-layouts: 5.97 us -> 22.3 us
    all_to_all x0 -> x1, starting transfers between devices: none -> 8.61 us  [body(): lax.all_to_all(jnp.tile(pair_local, repeats), 'seq', split_axis=0, concat...]
  transfers between devices with their start and end apart: 6 -> 6, of which waited for: 4 -> 4; matrix products, arithmetic and copies ran while one was open for 10% -> 11% of each run, Pallas kernels for 0% -> 0%
where the time goes in v1:
time: 597 us; the launch traced here: 594 us
  waiting for transfers between devices  357 us (60%)
  local copies, waits for them, and re-layouts  104 us (17%)
  other arithmetic  45.7 us (8%)
  matrix products  35.1 us (6%)
  starting transfers between devices  24.9 us (4%)
  between operations  14.3 us (2%)
  blocking collectives  12.6 us (2%)
    psum x1, waiting for transfers between devices, body(): lax.psum((local_qkv, local_out), ('dp', 'seq', 'head'))  263 us
    all_to_all x1, waiting for transfers between devices, body(): lax.all_to_all(jnp.tile(pair_local, repeats), 'seq', split_axis=0, concat...  47.8 us
    reduce_scatter x1, waiting for transfers between devices, body(): lax.psum_scatter(pair_sums.reshape(seq_length, local_heads, 2 * HD), 'seq...  41.2 us
    unnamed x36, local copies, waits for them, and re-layouts  22.3 us
    scatter-add x2, other arithmetic, scatter_step(): carried = carried.at[key_rows.reshape(-1)].add(both_parts)  20.1 us
    dot_general x4, matrix products, query_scores(): jnp.einsum('gqhe,gnkhe->ghqnk', query_blk, key_blk, preferred_element_typ...  15.6 us
    all_to_all x1, blocking collectives, body(): lax.all_to_all(packed, 'head', split_axis=1, concat_axis=0, tiled=True)  12.6 us
    reshape x4, local copies, waits for them, and re-layouts, query_scores(): return scores.reshape(scores.shape[0], scores.shape[1], scores.shape[2], -1)  12.4 us
  transfers between devices with their start and end apart: 6, of which 4 were waited for; matrix products, arithmetic and copies ran while one was open for 11% of the time, Pallas kernels for 0%

profile of v1, /device:TPU:2, one launch (start us, length us, event | category | flops | bytes accessed | tf_op | source)
XLA Modules:
  0.0 594.4 jit_solution(9020734415513466413)
XLA Ops:
  10.5 12.6 %all_to_all.68 = bf16[128,8,192]{0,2,1:T(8,128)(2,1)S(1)} all-to-all(bf16[128,8,192]{0,2,1:T(8,128)(2,1)S(1)} %bitcast.275), channel_id=1, replica_groups=mesh['dp'=4,'seq'=8,'head'=8] {'head'}, dimensions={1} | all-to-all | bytes 786432 | tf_op jit(solution)/shard_map/all_to_all | solution.py:58
  25.4 4.4 reduce.9
  29.9 5.8 reshape.399
  35.7 8.6 %all-to-all-start.1 = ((bf16[8,2,65536]{2,1,0:T(2,128)(2,1)}), bf16[8,2,65536]{2,1,0:T(2,128)(2,1)}, u32[]{:S(2)}, u32[]{:S(2)}) async-start(bf16[8,2,65536]{2,1,0:T(2,128)(2,1)} %reshape.399), calls=%async_computation.1 | async-start | bytes 4194304 | tf_op jit(solution)/shard_map/all_to_all | solution.py:63
  46.3 47.8 %all-to-all-done.1 = bf16[8,2,65536]{2,1,0:T(2,128)(2,1)} async-done(((bf16[8,2,65536]{2,1,0:T(2,128)(2,1)}), bf16[8,2,65536]{2,1,0:T(2,128)(2,1)}, u32[]{:S(2)}, u32[]{:S(2)}) %all-to-all-start.1) | async-done | bytes 2097184 | tf_op jit(solution)/shard_map/all_to_all | solution.py:63
  94.1 4.8 all-to-all-start.3
  98.9 6.8 %reshape.400 = bf16[8192,1,128]{2,1,0:T(2,128)(2,1)} reshape(bf16[8,2,65536]{2,1,0:T(2,128)(2,1)} %all-to-all-done.1) | data formatting | bytes 4194304
  105.7 3.8 copy.165
  110.1 40.2 %while.24 = (s32[]{:T(128)}, bf16[2,4,128,1,64]{2,4,1,3,0:T(8,128)(2,1)}, f32[2,4,1,128]{3,1,2,0:T(4,128)}, s32[2,4,9]{2,1,0:T(4,128)S(1)}, bf16[64,128,1,128]{3...) while((s32[]{:T(128)}, ...), condition=%wide.region_4.7_spmd, body=%wide.region_1.6_spmd.sunk | while | flops 156931296 | bytes 39141280 | solution.py:83
  111.5 3.4 gather_fusion
  118.7 3.6 fusion.80
  131.6 3.4 gather_fusion
  138.8 3.6 fusion.80
  154.4 86.1 %while.25 = (s32[]{:T(128)}, f32[64,128,1,128]{3,1,0,2:T(8,128)}, bf16[2,4,128,1,64]{2,4,1,3,0:T(8,128)(2,1)}, s32[2,4,9]{2,1,0:T(4,128)S(1)}, bf16[2,4,128,1,64...) while((s32[]{:T(128)}, f32[64,128,1,128]{3,1,0,2:T(8,128)}, ...), condition=%wide.region_8.11_spmd, body=%wide.region_6.10_spmd.sunk | while | flops 385783744 | bytes 64560684 | solution.py:148
  170.8 4.2 select_add_fusion.3
  187.4 10.1 %scatter_fusion = f32[64,128,128]{2,1,0:T(8,128)} fusion(f32[64,128,128]{2,1,0:T(8,128)} %bitcast.266, s32[36]{0:T(128)S(1)} %copy-done.24, f32[36,128,128]{2,1,0:T(8,128)} %bitcast.260), kind=kCustom, calls=%fused_computation.4.clone.1 | custom fusion | flops 589824 | bytes 7078032 | tf_op jit(solution)/shard_map/while/body/eval_jaxpr/scatter-add | solution.py:144
  214.0 4.2 select_add_fusion.3
  230.5 10.0 %scatter_fusion = f32[64,128,128]{2,1,0:T(8,128)} fusion(f32[64,128,128]{2,1,0:T(8,128)} %bitcast.266, s32[36]{0:T(128)S(1)} %copy-done.24, f32[36,128,128]{2,1,0:T(8,128)} %bitcast.260), kind=kCustom, calls=%fused_computation.4.clone.1 | custom fusion | flops 589824 | bytes 7078032 | tf_op jit(solution)/shard_map/while/body/eval_jaxpr/scatter-add | solution.py:144
  245.1 5.7 all-to-all-start.2
  251.1 41.2 %reduce-scatter.2.cloned.1.call-done = f32[1024,1,128]{2,1,0:T(1,128)} async-done(((f32[8192,1,128]{2,1,0:T(1,128)}), f32[1024,1,128]{2,1,0:T(1,128)}) %reduce-scatter.2.cloned.1.call-update) | async-done | bytes 524304 | tf_op jit(solution)/shard_map/reduce_scatter | solution.py:149
  295.7 4.0 reduce.11
  301.1 5.7 all-to-all-start.4
  308.8 4.7 all-to-all-done.4
  320.8 263.4 %all-reduce.3.cloned.1.call-done = (f32[512,1536]{0,1:T(8,128)}, f32[512,512]{0,1:T(8,128)}) async-done(((f32[512,1536]{0,1:T(8,128)}, f32[512,512]{0,1:T(8,128)}), (f32[512,1536]{0,1:T(8,128)}, f32[512,512]{0,1:T(8,128)})) %all-reduce.3.cloned.1.call-update) | async-done | bytes 4194320 | tf_op jit(solution)/shard_map/psum | solution.py:164
  (228 shorter events, 117.7 us)
Async XLA Ops:
  35.7 8.6 %copy-start.25 = (s32[1,64,9]{1,0,2:T(1,128)S(1)}, s32[1,64,9]{1,0,2:T(1,128)}, u32[]{:S(2)}) copy-start(s32[1,64,9]{1,0,2:T(1,128)} %param.17) | copy-start | bytes 6916
  35.7 8.8 %copy-start.6 = (bf16[512,512]{1,0:T(8,128)(2,1)S(1)}, bf16[512,512]{1,0:T(8,128)(2,1)}, u32[]{:S(2)}) copy-start(bf16[512,512]{1,0:T(8,128)(2,1)} %param.19) | copy-start | bytes 1572868
  35.7 8.8 %copy-start.17 = (bf16[1,128,512]{2,1,0:T(8,128)(2,1)S(1)}, bf16[1,128,512]{2,1,0:T(8,128)(2,1)}, u32[]{:S(2)}) copy-start(bf16[1,128,512]{2,1,0:T(8,128)(2,1)} %param.21) | copy-start | bytes 393220
  35.7 9.9 %copy-start.28 = (f32[8]{0:T(128)S(1)}, f32[8]{0:T(128)}, u32[]{:S(2)}) copy-start(f32[8]{0:T(128)} %param.20) | copy-start | bytes 100
  35.7 10.5 %copy-start.3 = (s32[1,8192]{1,0:T(1,128)S(1)}, s32[1,8192]{1,0:T(1,128)}, u32[]{:S(2)}) copy-start(s32[1,8192]{1,0:T(1,128)} %param.16) | copy-start | bytes 98308
  35.7 58.4 %all-to-all-start.1 = ((bf16[8,2,65536]{2,1,0:T(2,128)(2,1)}), bf16[8,2,65536]{2,1,0:T(2,128)(2,1)}, u32[]{:S(2)}, u32[]{:S(2)}) async-start(bf16[8,2,65536]{2,1,0:T(2,128)(2,1)} %reshape.399), calls=%async_computation.1 | async-start | bytes 4194304 | tf_op jit(solution)/shard_map/all_to_all | solution.py:63
  94.1 56.3 %all-to-all-start.3 = ((bf16[128,8,64]{0,2,1:T(8,128)(2,1)}), bf16[128,8,64]{0,2,1:T(8,128)(2,1)S(1)}, u32[]{:S(2)}, u32[]{:S(2)}) async-start(bf16[128,8,64]{0,2,1:T(8,128)(2,1)} %bitcast.51), calls=%async_computation.3 | async-start | bytes 262144 | tf_op jit(solution)/shard_map/all_to_all | solution.py:94
  98.9 193.4 %reduce-scatter.2.cloned.1.call-start = ((), (), s32[]{:S(2)}) async-start(), calls=%async_computation.6 | async-start | bytes 4718592 | tf_op jit(solution)/shard_map/reduce_scatter | solution.py:149
  118.7 5.4 copy-start.22
  124.1 3.1 copy-start.23
  124.1 3.1 copy-start.10
  138.8 5.4 copy-start.22
  144.2 3.1 copy-start.23
  154.4 6.5 %copy-start.8 = (bf16[2,4,128,1,64]{2,4,1,3,0:T(8,128)(2,1)}, bf16[2,4,128,1,64]{2,4,1,3,0:T(8,128)(2,1)S(1)}, u32[]{:S(2)}) copy-start(bf16[2,4,128,1,64]{2,4,1,3,0:T(8,128)(2,1)S(1)} %get-tuple-element.517) | copy-start | bytes 393220 | tf_op jit(solution)/shard_map/while
  187.4 10.1 %copy-start.21 = (f32[2,4,1,128]{3,1,2,0:T(4,128)S(1)}, f32[2,4,1,128]{3,1,2,0:T(4,128)}, u32[]{:S(2)}) copy-start(f32[2,4,1,128]{3,1,2,0:T(4,128)} %copy-done.20) | copy-start | bytes 12292 | tf_op jit(solution)/shard_map/while
  197.6 6.5 %copy-start.8 = (bf16[2,4,128,1,64]{2,4,1,3,0:T(8,128)(2,1)}, bf16[2,4,128,1,64]{2,4,1,3,0:T(8,128)(2,1)S(1)}, u32[]{:S(2)}) copy-start(bf16[2,4,128,1,64]{2,4,1,3,0:T(8,128)(2,1)S(1)} %get-tuple-element.517) | copy-start | bytes 393220 | tf_op jit(solution)/shard_map/while
  230.5 10.0 %copy-start.21 = (f32[2,4,1,128]{3,1,2,0:T(4,128)S(1)}, f32[2,4,1,128]{3,1,2,0:T(4,128)}, u32[]{:S(2)}) copy-start(f32[2,4,1,128]{3,1,2,0:T(4,128)} %copy-done.20) | copy-start | bytes 12292 | tf_op jit(solution)/shard_map/while
  241.5 9.3 %copy-start.16 = (bf16[2,4,128,1,64]{2,4,1,3,0:T(8,128)(2,1)S(1)}, bf16[2,4,128,1,64]{2,4,1,3,0:T(8,128)(2,1)}, u32[]{:S(2)}) copy-start(bf16[2,4,128,1,64]{2,4,1,3,0:T(8,128)(2,1)} %get-tuple-element.119) | copy-start | bytes 393220
  245.1 56.0 %all-to-all-start.2 = ((bf16[8,2,4096]{2,1,0:T(2,128)(2,1)}), bf16[8,2,4096]{2,1,0:T(2,128)(2,1)S(1)}, u32[]{:S(2)}, u32[]{:S(2)}) async-start(bf16[8,2,4096]{2,1,0:T(2,128)(2,1)} %reshape.401), calls=%async_computation.2 | async-start | bytes 262144 | tf_op jit(solution)/shard_map/all_to_all | solution.py:88
  295.7 11.8 %copy-start.18 = (bf16[1,128,512]{2,1,0:T(8,128)(2,1)S(1)}, bf16[1,128,512]{2,1,0:T(8,128)(2,1)}, u32[]{:S(2)}) copy-start(bf16[1,128,512]{2,1,0:T(8,128)(2,1)} %param.21) | copy-start | bytes 393220
  301.1 12.4 %all-to-all-start.4 = ((bf16[8,2,12288]{2,1,0:T(2,128)(2,1)}), bf16[8,2,12288]{2,1,0:T(2,128)(2,1)S(1)}, u32[]{:S(2)}, u32[]{:S(2)}) async-start(bf16[8,2,12288]{2,1,0:T(2,128)(2,1)} %reshape.403), calls=%async_computation.5 | async-start | bytes 786432 | tf_op jit(solution)/shard_map/all_to_all | solution.py:156
  306.8 277.4 %all-reduce.3.cloned.1.call-start = ((), (), s32[]{:S(2)}) async-start(), calls=%async_computation.7 | async-start | bytes 8388608 | tf_op jit(solution)/shard_map/psum | solution.py:164
  308.8 6.2 %copy-start.13 = (bf16[1,128,512]{2,1,0:T(8,128)(2,1)S(1)}, bf16[1,128,512]{2,1,0:T(8,128)(2,1)}, u32[]{:S(2)}) copy-start(bf16[1,128,512]{2,1,0:T(8,128)(2,1)} %param.15) | copy-start | bytes 393220
  308.8 6.2 %copy-start.27 = (f32[128]{0:T(128)S(1)}, f32[128]{0:T(128)}, u32[]{:S(2)}) copy-start(f32[128]{0:T(128)} %copy-done.26) | copy-start | bytes 1540
  (27 other events, 43.4 us)
Sparse Core Ops, SparseCore 0:
  240.7 51.5 reduce-scatter.1
  317.5 266.6 all-reduce.2
